TPU v7x, 32 devices: a whole 2x2x4 slice. The times are simulated.
32 devices in a mesh: user: 8 (over z, y), item: 4 (over x, core).
Axes of the slice: x: 2, y: 2, z: 4, core: 2. Of those that a mesh axis runs over, the one named last changes fastest.
Arguments:
- v_start: bfloat16 [32768, 64], P(('user', 'item')), may hold values from -6 to 6
- locked: bfloat16 [32768, 32], P(('user', 'item')), may hold values from -0.0625 to 0.0625
- tile_rows: int32 [32, 512], P(('user', 'item')), may hold values from 0 to 63, as said below
- tile_cols: int32 [32, 512], P(('user', 'item')), may hold values from 0 to 63
- tile_seeds: int32 [32, 512], P(('user', 'item')), may hold values from 0 to 1048575
- tile_count: int32 [32, 1], P(('user', 'item')), may hold values from 128 to 512, as said below
Outputs:
- u_factor: bfloat16 [65536, 64], P(('user', 'item'))
- v_next: float32 [32768, 64], P(('user', 'item'))
Inputs may be any that keep to these rules, and one draw needn't show every extreme that they name: `tile_count`: at most 512 live slots a device, and one device holds exactly 512. `tile_rows`: A device's slots name distinct (row, column) pairs.
All inputs are finite; a program needn't handle non-finite values.
Results may differ from a plain program's by a relative error of at most 0.0049.
Values may be sent and summed in bfloat16 or wider, within the bound.
A program may use at most 64 MiB of HBM per device.

v0:
```python
import functools

import jax
import jax.numpy as jnp
from jax import lax
from jax.experimental import pallas as pl
from jax.experimental.pallas import tpu as pltpu
from jax.sharding import PartitionSpec as P

TILE = 128
RB = 64
LIMIT = 16 << 20
GROUP = 16
SPAN = 32
SCALE = 1.0 / 1024.0
HIGH = lax.Precision.HIGHEST
NT = (((1,), (1,)), ((), ()))
NN = (((1,), (0,)), ((), ()))


def fill(seeds, tiles_ref, first, last, flip):
    a = lax.broadcasted_iota(jnp.int32, (TILE, TILE), 0)
    b = lax.broadcasted_iota(jnp.int32, (TILE, TILE), 1)
    base = (b * TILE + a if flip else a * TILE + b) * 40503

    def step(g, carry):
        for j in range(GROUP):
            s = g * GROUP + j
            h = base + seeds[0, s] * 9973
            h = h ^ (h >> 13)
            h = h * 1597334677
            h = h ^ (h >> 16)
            levels = ((h >> 8) & 255) - 128
            tiles_ref[s] = levels.astype(jnp.float32).astype(jnp.bfloat16)
        return carry

    lax.fori_loop(first, last, step, 0)


def fill_kernel(flip, seeds, tiles_ref):
    fill(seeds, tiles_ref, 0, tiles_ref.shape[0] // GROUP, flip)


def product_kernel(forward, places, count, x_ref, tiles_ref, out_ref, acc):
    blocks = out_ref.shape[0]
    live = count[0, 0]
    acc[...] = jnp.zeros_like(acc)

    def step(g, carry):
        for j in range(SPAN):
            s = g * SPAN + j
            row, col = places[0, s] >> 16, places[0, s] & 65535
            source, target = (col, row) if forward else (row, col)
            target = jnp.where(s < live, target, blocks)
            acc[target] += lax.dot_general(
                x_ref[source], tiles_ref[s], NN, preferred_element_type=jnp.float32
            )
        return carry

    lax.fori_loop(0, lax.div(live + (SPAN - 1), SPAN), step, 0)
    out_ref[...] = (acc[:blocks] * SCALE).astype(out_ref.dtype)


VMEM_SPEC = pl.BlockSpec(memory_space=pltpu.VMEM)
SMEM_SPEC = pl.BlockSpec(memory_space=pltpu.SMEM)


def product(forward, places, count, x, tiles, nblocks, dtype):
    width, tile = x.shape[1:]
    return pl.pallas_call(
        functools.partial(product_kernel, forward),
        name="forward" if forward else "backward",
        out_shape=jax.ShapeDtypeStruct((nblocks, width, tile), dtype),
        in_specs=[SMEM_SPEC, SMEM_SPEC, VMEM_SPEC, VMEM_SPEC],
        out_specs=VMEM_SPEC,
        scratch_shapes=[pltpu.VMEM((nblocks + 1, width, tile), jnp.float32)],
        compiler_params=pltpu.CompilerParams(vmem_limit_bytes=LIMIT),
    )(places, count, x, tiles)


def pack(tile_rows, tile_cols):
    return tile_rows * 65536 + tile_cols


def blocks_of(x):
    return x.reshape(-1, TILE, x.shape[1]).transpose(0, 2, 1)


def rows_of(blocks):
    return blocks.transpose(0, 2, 1).reshape(-1, blocks.shape[1])


MESH = pl.DeviceIdType.MESH
CHUNKS = 4


def place():
    user = lax.axis_index("user")
    return lax.div(user, 2), lax.rem(user, 2), lax.axis_index("item")


def plane():
    z, y, item = place()
    n = 2 * lax.axis_size("item")
    me = y * lax.axis_size("item") + item
    out = []
    for o in range(1, n):
        p = lax.rem(me + o, n)
        out.append({"user": 2 * z + lax.div(p, n // 2), "item": lax.rem(p, n // 2)})
    return n, me, out


def column():
    z, y, item = place()
    n = lax.axis_size("user") // 2
    return n, z, [{"user": 2 * lax.rem(z + o, n) + y, "item": item} for o in range(1, n)]


def facing():
    z, y, item = place()
    return {"user": 2 * z + 1 - y, "item": item}


def meet(devices):
    barrier = pltpu.get_barrier_semaphore()
    for device in devices:
        pl.semaphore_signal(barrier, inc=1, device_id=device, device_id_type=MESH)
    pl.semaphore_wait(barrier, len(devices))


def remote(src, dst, send, recv, device):
    return pltpu.make_async_remote_copy(
        src_ref=src, dst_ref=dst, send_sem=send, recv_sem=recv, device_id=device,
        device_id_type=MESH,
    )


def sum_over(group, value, slots, send, recv, meanwhile=lambda: None):
    n, me, devices = group
    slots[me] = value
    copies = [
        remote(slots.at[me], slots.at[me], send.at[o], recv.at[o], device)
        for o, device in enumerate(devices)
    ]
    for copy in copies:
        copy.start()
    meanwhile()
    for copy in copies:
        copy.wait()
    total = slots[0]
    for i in range(1, n):
        total = total + slots[i]
    return total


def gather_kernel(
    seeds, cat_ref, v_ref, stats_ref, tiles_ref,
    slots_p, slots_c, sp, rp, sc, rc, sz, rz, sy, ry,
):
    groups = tiles_ref.shape[0] // GROUP
    parts = 2 + lax.axis_size("user") // 2 - 1

    def some(i):
        fill(seeds, tiles_ref, groups * i // parts, groups * (i + 1) // parts, True)

    nlock = stats_ref.shape[0]
    width = v_ref.shape[1]
    meet(plane()[2] + column()[2])
    lock = cat_ref[:nlock]
    stats = lax.dot_general(lock, cat_ref[...], NT, preferred_element_type=jnp.float32)
    stats = sum_over(plane(), stats, slots_p, sp, rp, lambda: some(0))
    stats = sum_over(column(), stats, slots_c, sc, rc, lambda: some(1))
    stats_ref[...] = stats
    projt = stats.T[nlock : nlock + width]
    own = cat_ref.shape[1] // TILE
    n, z, devices = column()
    y = place()[1]

    def block(o):
        at = (2 * lax.rem(z + n - o, n) + y) * own
        return v_ref.at[pl.ds(at, own)]

    for j in range(own):
        at = slice(j * TILE, (j + 1) * TILE)
        v = cat_ref[nlock : nlock + width, at].astype(jnp.float32)
        part = jnp.dot(projt, cat_ref[:nlock, at].astype(jnp.float32), precision=HIGH)
        v_ref[(2 * z + y) * own + j] = (v - part).astype(v_ref.dtype)
    down = [
        remote(block(0), block(0), sz.at[o], rz.at[o], device)
        for o, device in enumerate(devices)
    ]
    over = [remote(block(o), block(o), sy.at[o], ry.at[o], facing()) for o in range(n)]
    for copy in down:
        copy.start()
    over[0].start()
    for o in range(1, n):
        some(1 + o)
        down[o - 1].wait_recv()
        over[o].start()
    for copy in down:
        copy.wait_send()
    for copy in over:
        copy.wait()


def user_sum_kernel(seeds, part_ref, u_ref, tiles_ref, near, pair, far, sem):
    groups = tiles_ref.shape[0] // GROUP
    early, late = groups // 32, groups * 6 // 32
    me = lax.axis_index("item")
    side = lax.rem(me, 2)
    sibling = {"item": me + 1 - 2 * side}
    across = {"item": lax.rem(me + 2, 4)}
    half = part_ref.shape[0] // 2
    size = half // CHUNKS
    meet([sibling, across])

    def copies(step, src, src_at, dst, dst_at, device):
        return [
            remote(
                src.at[pl.ds(src_at + k * size, size)],
                dst.at[pl.ds(dst_at + k * size, size)],
                sem.at[2 * step, k],
                sem.at[2 * step + 1, k],
                device,
            )
            for k in range(CHUNKS)
        ]

    give = copies(0, part_ref, (1 - side) * half, near, 0, sibling)
    swap = copies(1, pair, 0, far, 0, across)
    back = copies(2, u_ref, side * half, u_ref, side * half, sibling)
    for copy in give:
        copy.start()
    for k in range(CHUNKS):
        give[k].wait_recv()
        at = pl.ds(k * size, size)
        own = part_ref[pl.ds(side * half + k * size, size)].astype(jnp.float32)
        pair[at] = (own + near[at].astype(jnp.float32)).astype(pair.dtype)
        swap[k].start()
        fill(seeds, tiles_ref, k * early, (k + 1) * early, False)
    for k in range(CHUNKS):
        first = CHUNKS * early + k * late
        fill(seeds, tiles_ref, first, first + late, False)
        swap[k].wait_recv()
        at = pl.ds(k * size, size)
        total = pair[at].astype(jnp.float32) + far[at].astype(jnp.float32)
        u_ref[pl.ds(side * half + k * size, size)] = total.astype(u_ref.dtype)
        back[k].start()
    fill(seeds, tiles_ref, CHUNKS * (early + late), groups, False)
    for k in range(CHUNKS):
        give[k].wait_send()
        swap[k].wait_send()
        back[k].wait()


def finish_kernel(
    items, part_ref, lock_ref, stats_ref, v_ref,
    near, pair, land, slots_p, slots_c, sy, ry, sz, rz, sp, rp, sc, rc,
):
    nlock = stats_ref.shape[0]
    own, width, tile = land.shape[1:]
    n, z, devices = column()
    y = place()[1]
    meet(plane()[2] + devices)

    def piece(t, side):
        return pl.ds((2 * lax.rem(z + 1 + t, n) + side) * own, own)

    over = [
        remote(part_ref.at[piece(t, 1 - y)], near.at[t], sy.at[t], ry.at[t], facing())
        for t in range(n)
    ]
    down = [
        remote(pair.at[t], land.at[t], sz.at[t], rz.at[t], device)
        for t, device in enumerate(devices)
    ]
    for copy in over:
        copy.start()
    for t in range(n):
        over[t].wait_recv()
        both = part_ref[piece(t, y)].astype(jnp.float32) + near[t].astype(jnp.float32)
        if t < n - 1:
            pair[t] = both.astype(pair.dtype)
            down[t].start()
    for copy in over:
        copy.wait_send()
    for copy in down:
        copy.wait()
    back, square = [], jnp.zeros((width, tile), jnp.float32)
    rows = nlock + 8
    sums = jnp.zeros((rows, width), jnp.float32)
    for j in range(own):
        b = part_ref[(2 * z + y) * own + j].astype(jnp.float32) + near[n - 1, j].astype(
            jnp.float32
        )
        for t in range(n - 1):
            b = b + land[t, j].astype(jnp.float32)
        back.append(b)
        square = square + b * b
        lock = lock_ref[:rows, j * tile : (j + 1) * tile].astype(jnp.float32)
        sums = sums + lax.dot_general(
            lock, b, NT, precision=HIGH, preferred_element_type=jnp.float32
        )
    squares = lax.dot_general(
        jnp.ones((rows, tile), jnp.float32), square, NT, precision=HIGH,
        preferred_element_type=jnp.float32,
    )
    lane = lax.broadcasted_iota(jnp.int32, (rows, width), 0)
    sums = jnp.where(lane >= nlock, squares, sums)
    sums = jnp.concatenate([sums, jnp.zeros((rows, tile - width), jnp.float32)], axis=1)
    sums = sum_over(plane(), sums, slots_p, sp, rp)
    sums = sum_over(column(), sums, slots_c, sc, rc)
    sums = sums.T[:width]
    proj2, backsq = sums[:, :nlock], sums[:, nlock : nlock + 1]
    gram = stats_ref[:, :nlock]
    crossed = jnp.dot(proj2, gram, precision=HIGH) - 2.0 * proj2
    colsq = backsq + jnp.sum(proj2 * crossed, axis=1, keepdims=True)
    scale = 1.0 / jnp.sqrt(jnp.maximum(colsq, 0.0) / items + 1e-06)
    for j in range(own):
        lock = lock_ref[:nlock, j * tile : (j + 1) * tile].astype(jnp.float32)
        rest = back[j] - jnp.dot(proj2, lock, precision=HIGH)
        v_ref[j * tile : (j + 1) * tile, :] = (rest * scale).T


def comm_call(kernel, name, key, out_shape, scratch, *args):
    vmem = pl.BlockSpec(memory_space=pltpu.VMEM)
    return pl.pallas_call(
        kernel,
        name=name,
        out_shape=out_shape,
        in_specs=[SMEM_SPEC if x.dtype == jnp.int32 else vmem for x in args],
        out_specs=jax.tree.map(lambda _: vmem, out_shape),
        scratch_shapes=scratch,
        compiler_params=pltpu.CompilerParams(
            collective_id=key, has_side_effects=True, vmem_limit_bytes=LIMIT
        ),
    )(*args)


def sems(*shape):
    return pltpu.SemaphoreType.DMA(shape)


def remote_plan(v_start, locked, tile_rows, tile_cols, tile_seeds, tile_count):
    n_user, n_item = lax.axis_size("user"), lax.axis_size("item")
    shard, width = v_start.shape
    nlock = locked.shape[1]
    nblocks = shard * n_user // TILE
    pad = jnp.zeros((shard, TILE - nlock - width), v_start.dtype)
    cat = jnp.concatenate([locked, v_start, pad], axis=1).T
    slab = (nblocks, width, TILE)
    wide, deep = 2 * n_item, n_user // 2
    pair = [sems(wide - 1)] * 2 + [sems(deep - 1)] * 2
    vblocks, stats, tiles = comm_call(
        gather_kernel,
        "gather",
        0,
        (
            jax.ShapeDtypeStruct(slab, jnp.bfloat16),
            jax.ShapeDtypeStruct((nlock, TILE), jnp.float32),
            jax.ShapeDtypeStruct((tile_seeds.shape[1], TILE, TILE), jnp.bfloat16),
        ),
        [
            pltpu.VMEM((wide, nlock, TILE), jnp.float32),
            pltpu.VMEM((deep, nlock, TILE), jnp.float32),
        ]
        + pair
        + [sems(deep - 1)] * 2
        + [sems(deep)] * 2,
        tile_seeds,
        cat,
    )
    places = pack(tile_rows, tile_cols)
    upart = product(True, places, tile_count, vblocks, tiles, RB, jnp.bfloat16)
    half = pltpu.VMEM((RB // 2, width, TILE), jnp.bfloat16)
    ublocks, tiles = comm_call(
        user_sum_kernel,
        "user_sum",
        1,
        (
            jax.ShapeDtypeStruct((RB, width, TILE), jnp.bfloat16),
            jax.ShapeDtypeStruct((tile_seeds.shape[1], TILE, TILE), jnp.bfloat16),
        ),
        [half, half, half, sems(6, CHUNKS)],
        tile_seeds,
        upart,
    )
    wpart = product(False, places, tile_count, ublocks, tiles, nblocks, jnp.bfloat16)
    per = RB // n_item
    u_factor = rows_of(lax.dynamic_slice_in_dim(ublocks, lax.axis_index("item") * per, per, 0))
    only = jnp.concatenate([locked, jnp.zeros((shard, TILE - nlock), locked.dtype)], axis=1).T
    v_next = comm_call(
        functools.partial(finish_kernel, float(shard * n_user * n_item)),
        "finish",
        2,
        jax.ShapeDtypeStruct((shard, width), jnp.float32),
        [
            pltpu.VMEM((deep, nblocks // n_user, width, TILE), jnp.bfloat16),
            pltpu.VMEM((deep - 1, nblocks // n_user, width, TILE), jnp.bfloat16),
            pltpu.VMEM((deep - 1, nblocks // n_user, width, TILE), jnp.bfloat16),
            pltpu.VMEM((wide, nlock + 8, TILE), jnp.float32),
            pltpu.VMEM((deep, nlock + 8, TILE), jnp.float32),
        ]
        + [sems(deep)] * 2
        + [sems(deep - 1)] * 2
        + pair,
        wpart,
        only,
        stats,
    )
    return (u_factor, v_next)


def on_device(v_start, locked, tile_rows, tile_cols, tile_seeds, tile_count):
    if v_start.shape[0] % TILE == 0 and lax.axis_size("item") == 4 and lax.axis_size("user") % 2 == 0:
        return remote_plan(v_start, locked, tile_rows, tile_cols, tile_seeds, tile_count)
    both = ("user", "item")
    lockf = locked.astype(jnp.float32)
    nlock = locked.shape[1]
    n_user, n_item = lax.axis_size("user"), lax.axis_size("item")
    slab = v_start.shape[0] * n_user
    stats = jnp.dot(
        locked.T, jnp.concatenate([v_start, locked], axis=1), preferred_element_type=jnp.float32
    )
    stats = lax.psum(stats, both)
    proj, gram = stats[:, :-nlock], stats[:, -nlock:]
    deflated = (v_start.astype(jnp.float32) - jnp.dot(lockf, proj, precision=HIGH)).astype(
        jnp.bfloat16
    )
    vslab = lax.all_gather(deflated, "user", axis=0, tiled=True)
    places = pack(tile_rows, tile_cols)
    flipped, tiles = [
        pl.pallas_call(
            functools.partial(fill_kernel, flip),
            name="fill",
            out_shape=jax.ShapeDtypeStruct((tile_seeds.shape[1], TILE, TILE), jnp.bfloat16),
            in_specs=[SMEM_SPEC],
            out_specs=VMEM_SPEC,
            compiler_params=pltpu.CompilerParams(vmem_limit_bytes=LIMIT),
        )(tile_seeds)
        for flip in (True, False)
    ]
    upart = product(True, places, tile_count, blocks_of(vslab), flipped, RB, jnp.float32)
    ublocks = lax.psum(upart, "item").astype(jnp.bfloat16)
    per = RB // n_item
    u_factor = rows_of(lax.dynamic_slice_in_dim(ublocks, lax.axis_index("item") * per, per, 0))
    wpart = product(False, places, tile_count, ublocks, tiles, slab // TILE, jnp.float32)
    back = lax.psum_scatter(rows_of(wpart), "user", scatter_dimension=0, tiled=True)
    sums = jnp.concatenate(
        [jnp.dot(lockf.T, back, precision=HIGH), jnp.sum(back * back, axis=0)[None]], axis=0
    )
    sums = lax.psum(sums, both)
    proj2, backsq = sums[:-1], sums[-1]
    rest = back - jnp.dot(lockf, proj2, precision=HIGH)
    crossed = jnp.dot(gram, proj2, precision=HIGH) - 2.0 * proj2
    colsq = jnp.maximum(backsq + jnp.sum(proj2 * crossed, axis=0), 0.0)
    v_next = rest / jnp.sqrt(colsq / (slab * n_item) + 1e-06)
    return (u_factor, v_next)


def solution(mesh):
    spec = P(("user", "item"), None)
    return jax.shard_map(
        on_device, mesh=mesh, in_specs=(spec,) * 6, out_specs=(spec, spec), check_vma=False
    )
```

profile of v0, /device:TPU:0, one launch (start us, length us, event | category | flops | bytes accessed | tf_op | source)
XLA Modules:
  0.0 92.7 jit_solution(15731906876418200197)
XLA Ops:
  0.6 0.1 pad.3.clone
  0.7 1.1 %pad_bitcast_fusion = (bf16[128,1024]{1,0:T(8,128)(2,1)S(1)}, bf16[128,1024]{1,0:T(8,128)(2,1)S(1)}) fusion(bf16[1024,32]{0,1:T(8,128)(2,1)} %param.7, bf16[128]{0:T(256)(128)(2,1)S(1)} %pad.3.clone, bf16[1024,64]{0,1:T(8,128)(2,1)} %param.6), kind=kLoop, calls=%fused_computation.2 | loop fusion | flops 786432 | bytes 721152 | tf_op jit(solution)/shard_map/transpose | solution.py:391
  1.8 0.0 copy-start
  1.8 0.7 copy-done
  2.5 32.1 %gather.1 = (bf16[64,64,128]{2,1,0:T(8,128)(2,1)S(1)}, f32[32,128]{1,0:T(8,128)S(1)}, bf16[512,128,128]{2,1,0:T(8,128)(2,1)S(1)}) custom-call(s32[1,512]{1,0:T(1,128)S(1)} %copy-done, bf16[128,1024]{1,0:T(8,128)(2,1)S(1)} %get-tuple-element.17.cat_ref), custom_call_target="tpu_custom_call" | custom-call | tf_op jit(solution)/shard_map/gather/pallas_call | solution.py:327
  34.6 0.7 multiply_add_fusion.places
  36.0 3.3 %forward.1.part_ref = bf16[64,64,128]{2,1,0:T(8,128)(2,1)S(1)} custom-call(s32[1,512]{1,0:T(1,128)S(1)} %multiply_add_fusion.places, s32[1,1]{1,0:T(1,128)S(6)} %copy.13.count, bf16[64,64,128]{2,1,0:T(8,128)(2,1)S(1)} %get-tuple-element.7.x_ref, bf16[512,128,128]{2,1,0:T(8,128)(2,1)S(1)} %get-tuple-element.8.tiles_ref), custom_call_target="tpu_custom_call" | custom-call | tf_op jit(solution)/shard_map/forward/pallas_call | solution.py:70
  39.4 17.8 %user_sum.1 = (bf16[64,64,128]{2,1,0:T(8,128)(2,1)S(1)}, bf16[512,128,128]{2,1,0:T(8,128)(2,1)S(1)}) custom-call(s32[1,512]{1,0:T(1,128)S(1)} %copy-done, bf16[64,64,128]{2,1,0:T(8,128)(2,1)S(1)} %forward.1.part_ref), custom_call_target="tpu_custom_call" | custom-call | tf_op jit(solution)/shard_map/user_sum/pallas_call | solution.py:327
  57.2 3.4 %backward.1.part_ref = bf16[64,64,128]{2,1,0:T(8,128)(2,1)S(1)} custom-call(s32[1,512]{1,0:T(1,128)S(1)} %multiply_add_fusion.places, s32[1,1]{1,0:T(1,128)S(6)} %copy.13.count, bf16[64,64,128]{2,1,0:T(8,128)(2,1)S(1)} %get-tuple-element.9.x_ref, bf16[512,128,128]{2,1,0:T(8,128)(2,1)S(1)} %get-tuple-element.10.tiles_ref), custom_call_target="tpu_custom_call" | custom-call | tf_op jit(solution)/shard_map/backward/pallas_call | solution.py:70
  60.6 30.4 %finish.1 = f32[1024,64]{1,0:T(8,128)S(1)} custom-call(bf16[64,64,128]{2,1,0:T(8,128)(2,1)S(1)} %backward.1.part_ref, bf16[128,1024]{1,0:T(8,128)(2,1)S(1)} %get-tuple-element.16.lock_ref, f32[32,128]{1,0:T(8,128)S(1)} %get-tuple-element.11.stats_ref), custom_call_target="tpu_custom_call" | custom-call | tf_op jit(solution)/shard_map/finish/pallas_call | solution.py:327
  91.1 0.9 copy.10
  92.0 0.7 copy_bitcast_fusion
  (1 shorter events, 0.0 us)
Async XLA Ops:
  1.8 0.7 copy-start
where the time goes:
time: 93.1 us; the launch traced here: 92.7 us
  Pallas kernels  87.2 us (94%)
  local copies, waits for them, and re-layouts  2.38 us (3%)
  other arithmetic  1.79 us (2%)
  between operations  1.34 us (1%)
    pallas_call x3, Pallas kernels, comm_call(): pl.pallas_call(kernel, name=name, out_shape=out_shape, in_specs=[SMEM_SPE...  80.4 us
    pallas_call x2, Pallas kernels, product(): pl.pallas_call(functools.partial(product_kernel, forward), name='forward'...  6.79 us

commit v1 on v0

--- a/solution.py
+++ b/solution.py
@@ -11,7 +11,7 @@
 RB = 64
 LIMIT = 16 << 20
 GROUP = 16
-SPAN = 32
+SPAN = 64
 SCALE = 1.0 / 1024.0
 HIGH = lax.Precision.HIGHEST
 NT = (((1,), (1,)), ((), ()))
@@ -158,10 +158,11 @@
     slots_p, slots_c, sp, rp, sc, rc, sz, rz, sy, ry,
 ):
     groups = tiles_ref.shape[0] // GROUP
-    parts = 2 + lax.axis_size("user") // 2 - 1
+    parts = lax.axis_size("user")
 
     def some(i):
-        fill(seeds, tiles_ref, groups * i // parts, groups * (i + 1) // parts, True)
+        first, last = (i, i + 1) if i < 2 else (2 * i - 2, 2 * i)
+        fill(seeds, tiles_ref, groups * first // parts, groups * last // parts, True)
 
     nlock = stats_ref.shape[0]
     width = v_ref.shape[1]

time: 93.1 us -> 94.7 us (1.017)
  Pallas kernels: 87.2 us -> 89 us
    pallas_call x3, Pallas kernels: 80.4 us -> 83.1 us  [comm_call(): pl.pallas_call(kernel, name=name, out_shape=out_shape, in_specs=[SMEM_SPE...]
where the time goes in v1:
time: 94.7 us; the launch traced here: 94.6 us
  Pallas kernels  89 us (94%)
  local copies, waits for them, and re-layouts  2.38 us (3%)
  other arithmetic  1.79 us (2%)
  between operations  1.35 us (1%)
    pallas_call x3, Pallas kernels, comm_call(): pl.pallas_call(kernel, name=name, out_shape=out_shape, in_specs=[SMEM_SPE...  83.1 us
    pallas_call x2, Pallas kernels, product(): pl.pallas_call(functools.partial(product_kernel, forward), name='forward'...  5.98 us

profile of v1, /device:TPU:0, one launch (start us, length us, event | category | flops | bytes accessed | tf_op | source)
XLA Modules:
  0.0 94.6 jit_solution(13707250396610956022)
XLA Ops:
  0.6 0.1 pad.3.clone
  0.7 1.1 %pad_bitcast_fusion = (bf16[128,1024]{1,0:T(8,128)(2,1)S(1)}, bf16[128,1024]{1,0:T(8,128)(2,1)S(1)}) fusion(bf16[1024,32]{0,1:T(8,128)(2,1)} %param.7, bf16[128]{0:T(256)(128)(2,1)S(1)} %pad.3.clone, bf16[1024,64]{0,1:T(8,128)(2,1)} %param.6), kind=kLoop, calls=%fused_computation.2 | loop fusion | flops 786432 | bytes 721152 | tf_op jit(solution)/shard_map/transpose | solution.py:392
  1.8 0.0 copy-start
  1.8 0.7 copy-done
  2.5 32.5 %gather.1 = (bf16[64,64,128]{2,1,0:T(8,128)(2,1)S(1)}, f32[32,128]{1,0:T(8,128)S(1)}, bf16[512,128,128]{2,1,0:T(8,128)(2,1)S(1)}) custom-call(s32[1,512]{1,0:T(1,128)S(1)} %copy-done, bf16[128,1024]{1,0:T(8,128)(2,1)S(1)} %get-tuple-element.17.cat_ref), custom_call_target="tpu_custom_call" | custom-call | tf_op jit(solution)/shard_map/gather/pallas_call | solution.py:328
  35.0 0.7 multiply_add_fusion.places
  36.4 2.9 %forward.1.part_ref = bf16[64,64,128]{2,1,0:T(8,128)(2,1)S(1)} custom-call(s32[1,512]{1,0:T(1,128)S(1)} %multiply_add_fusion.places, s32[1,1]{1,0:T(1,128)S(6)} %copy.13.count, bf16[64,64,128]{2,1,0:T(8,128)(2,1)S(1)} %get-tuple-element.7.x_ref, bf16[512,128,128]{2,1,0:T(8,128)(2,1)S(1)} %get-tuple-element.8.tiles_ref), custom_call_target="tpu_custom_call" | custom-call | tf_op jit(solution)/shard_map/forward/pallas_call | solution.py:70
  39.3 16.7 %user_sum.1 = (bf16[64,64,128]{2,1,0:T(8,128)(2,1)S(1)}, bf16[512,128,128]{2,1,0:T(8,128)(2,1)S(1)}) custom-call(s32[1,512]{1,0:T(1,128)S(1)} %copy-done, bf16[64,64,128]{2,1,0:T(8,128)(2,1)S(1)} %forward.1.part_ref), custom_call_target="tpu_custom_call" | custom-call | tf_op jit(solution)/shard_map/user_sum/pallas_call | solution.py:328
  56.1 3.0 %backward.1.part_ref = bf16[64,64,128]{2,1,0:T(8,128)(2,1)S(1)} custom-call(s32[1,512]{1,0:T(1,128)S(1)} %multiply_add_fusion.places, s32[1,1]{1,0:T(1,128)S(6)} %copy.13.count, bf16[64,64,128]{2,1,0:T(8,128)(2,1)S(1)} %get-tuple-element.9.x_ref, bf16[512,128,128]{2,1,0:T(8,128)(2,1)S(1)} %get-tuple-element.10.tiles_ref), custom_call_target="tpu_custom_call" | custom-call | tf_op jit(solution)/shard_map/backward/pallas_call | solution.py:70
  59.1 33.8 %finish.1 = f32[1024,64]{1,0:T(8,128)S(1)} custom-call(bf16[64,64,128]{2,1,0:T(8,128)(2,1)S(1)} %backward.1.part_ref, bf16[128,1024]{1,0:T(8,128)(2,1)S(1)} %get-tuple-element.16.lock_ref, f32[32,128]{1,0:T(8,128)S(1)} %get-tuple-element.11.stats_ref), custom_call_target="tpu_custom_call" | custom-call | tf_op jit(solution)/shard_map/finish/pallas_call | solution.py:328
  92.9 0.9 copy.10
  93.8 0.7 copy_bitcast_fusion
  (1 shorter events, 0.0 us)
Async XLA Ops:
  1.8 0.7 copy-start

commit v2 on v1

--- a/solution.py
+++ b/solution.py
@@ -91,7 +91,7 @@
 
 
 MESH = pl.DeviceIdType.MESH
-CHUNKS = 4
+CHUNKS = 8
 
 
 def place():
@@ -206,7 +206,7 @@
 
 def user_sum_kernel(seeds, part_ref, u_ref, tiles_ref, near, pair, far, sem):
     groups = tiles_ref.shape[0] // GROUP
-    early, late = groups // 32, groups * 6 // 32
+    early, late = groups // 32, groups * 3 // 32
     me = lax.axis_index("item")
     side = lax.rem(me, 2)
     sibling = {"item": me + 1 - 2 * side}

time: 94.7 us -> 93.9 us (level)
    pallas_call x3, Pallas kernels: 83.1 us -> 80.8 us  [comm_call(): pl.pallas_call(kernel, name=name, out_shape=out_shape, in_specs=[SMEM_SPE...]
    pallas_call x2, Pallas kernels: 5.98 us -> 7.44 us  [product(): pl.pallas_call(functools.partial(product_kernel, forward), name='forward'...]
where the time goes in v2:
time: 93.9 us; the launch traced here: 93.7 us
  Pallas kernels  88.2 us (94%)
  local copies, waits for them, and re-layouts  2.38 us (3%)
  other arithmetic  1.79 us (2%)
  between operations  1.35 us (1%)
    pallas_call x3, Pallas kernels, comm_call(): pl.pallas_call(kernel, name=name, out_shape=out_shape, in_specs=[SMEM_SPE...  80.8 us
    pallas_call x2, Pallas kernels, product(): pl.pallas_call(functools.partial(product_kernel, forward), name='forward'...  7.44 us

profile of v2, /device:TPU:0, one launch (start us, length us, event | category | flops | bytes accessed | tf_op | source)
XLA Modules:
  0.0 93.7 jit_solution(10341375863614564090)
XLA Ops:
  0.6 0.1 pad.3.clone
  0.7 1.1 %pad_bitcast_fusion = (bf16[128,1024]{1,0:T(8,128)(2,1)S(1)}, bf16[128,1024]{1,0:T(8,128)(2,1)S(1)}) fusion(bf16[1024,32]{0,1:T(8,128)(2,1)} %param.7, bf16[128]{0:T(256)(128)(2,1)S(1)} %pad.3.clone, bf16[1024,64]{0,1:T(8,128)(2,1)} %param.6), kind=kLoop, calls=%fused_computation.2 | loop fusion | flops 786432 | bytes 721152 | tf_op jit(solution)/shard_map/transpose | solution.py:392
  1.8 0.0 copy-start
  1.8 0.7 copy-done
  2.5 32.5 %gather.1 = (bf16[64,64,128]{2,1,0:T(8,128)(2,1)S(1)}, f32[32,128]{1,0:T(8,128)S(1)}, bf16[512,128,128]{2,1,0:T(8,128)(2,1)S(1)}) custom-call(s32[1,512]{1,0:T(1,128)S(1)} %copy-done, bf16[128,1024]{1,0:T(8,128)(2,1)S(1)} %get-tuple-element.17.cat_ref), custom_call_target="tpu_custom_call" | custom-call | tf_op jit(solution)/shard_map/gather/pallas_call | solution.py:328
  35.0 0.7 multiply_add_fusion.places
  36.4 3.7 %forward.1.part_ref = bf16[64,64,128]{2,1,0:T(8,128)(2,1)S(1)} custom-call(s32[1,512]{1,0:T(1,128)S(1)} %multiply_add_fusion.places, s32[1,1]{1,0:T(1,128)S(6)} %copy.13.count, bf16[64,64,128]{2,1,0:T(8,128)(2,1)S(1)} %get-tuple-element.7.x_ref, bf16[512,128,128]{2,1,0:T(8,128)(2,1)S(1)} %get-tuple-element.8.tiles_ref), custom_call_target="tpu_custom_call" | custom-call | tf_op jit(solution)/shard_map/forward/pallas_call | solution.py:70
  40.1 16.9 %user_sum.1 = (bf16[64,64,128]{2,1,0:T(8,128)(2,1)S(1)}, bf16[512,128,128]{2,1,0:T(8,128)(2,1)S(1)}) custom-call(s32[1,512]{1,0:T(1,128)S(1)} %copy-done, bf16[64,64,128]{2,1,0:T(8,128)(2,1)S(1)} %forward.1.part_ref), custom_call_target="tpu_custom_call" | custom-call | tf_op jit(solution)/shard_map/user_sum/pallas_call | solution.py:328
  57.0 3.8 %backward.1.part_ref = bf16[64,64,128]{2,1,0:T(8,128)(2,1)S(1)} custom-call(s32[1,512]{1,0:T(1,128)S(1)} %multiply_add_fusion.places, s32[1,1]{1,0:T(1,128)S(6)} %copy.13.count, bf16[64,64,128]{2,1,0:T(8,128)(2,1)S(1)} %get-tuple-element.9.x_ref, bf16[512,128,128]{2,1,0:T(8,128)(2,1)S(1)} %get-tuple-element.10.tiles_ref), custom_call_target="tpu_custom_call" | custom-call | tf_op jit(solution)/shard_map/backward/pallas_call | solution.py:70
  60.8 31.3 %finish.1 = f32[1024,64]{1,0:T(8,128)S(1)} custom-call(bf16[64,64,128]{2,1,0:T(8,128)(2,1)S(1)} %backward.1.part_ref, bf16[128,1024]{1,0:T(8,128)(2,1)S(1)} %get-tuple-element.16.lock_ref, f32[32,128]{1,0:T(8,128)S(1)} %get-tuple-element.11.stats_ref), custom_call_target="tpu_custom_call" | custom-call | tf_op jit(solution)/shard_map/finish/pallas_call | solution.py:328
  92.1 0.9 copy.10
  93.0 0.7 copy_bitcast_fusion
  (1 shorter events, 0.0 us)
Async XLA Ops:
  1.8 0.7 copy-start

commit v3 on v1

--- a/solution.py
+++ b/solution.py
@@ -11,7 +11,7 @@
 RB = 64
 LIMIT = 16 << 20
 GROUP = 16
-SPAN = 64
+SPAN = 128
 SCALE = 1.0 / 1024.0
 HIGH = lax.Precision.HIGHEST
 NT = (((1,), (1,)), ((), ()))

time: 94.7 us -> 94.6 us (level)
  no operation moved by 1% of the time
where the time goes in v3:
time: 94.6 us; the launch traced here: 95.2 us
  Pallas kernels  89.7 us (95%)
  local copies, waits for them, and re-layouts  2.38 us (3%)
  other arithmetic  1.79 us (2%)
  between operations  1.35 us (1%)
    pallas_call x3, Pallas kernels, comm_call(): pl.pallas_call(kernel, name=name, out_shape=out_shape, in_specs=[SMEM_SPE...  82.9 us
    pallas_call x2, Pallas kernels, product(): pl.pallas_call(functools.partial(product_kernel, forward), name='forward'...  6.86 us

profile of v3, /device:TPU:0, one launch (start us, length us, event | category | flops | bytes accessed | tf_op | source)
XLA Modules:
  0.0 95.2 jit_solution(11981534257622470430)
XLA Ops:
  0.6 0.1 pad.3.clone
  0.7 1.1 %pad_bitcast_fusion = (bf16[128,1024]{1,0:T(8,128)(2,1)S(1)}, bf16[128,1024]{1,0:T(8,128)(2,1)S(1)}) fusion(bf16[1024,32]{0,1:T(8,128)(2,1)} %param.7, bf16[128]{0:T(256)(128)(2,1)S(1)} %pad.3.clone, bf16[1024,64]{0,1:T(8,128)(2,1)} %param.6), kind=kLoop, calls=%fused_computation.2 | loop fusion | flops 786432 | bytes 721152 | tf_op jit(solution)/shard_map/transpose | solution.py:392
  1.8 0.0 copy-start
  1.8 0.7 copy-done
  2.5 32.5 %gather.1 = (bf16[64,64,128]{2,1,0:T(8,128)(2,1)S(1)}, f32[32,128]{1,0:T(8,128)S(1)}, bf16[512,128,128]{2,1,0:T(8,128)(2,1)S(1)}) custom-call(s32[1,512]{1,0:T(1,128)S(1)} %copy-done, bf16[128,1024]{1,0:T(8,128)(2,1)S(1)} %get-tuple-element.17.cat_ref), custom_call_target="tpu_custom_call" | custom-call | tf_op jit(solution)/shard_map/gather/pallas_call | solution.py:328
  35.0 0.7 multiply_add_fusion.places
  36.4 3.4 %forward.1.part_ref = bf16[64,64,128]{2,1,0:T(8,128)(2,1)S(1)} custom-call(s32[1,512]{1,0:T(1,128)S(1)} %multiply_add_fusion.places, s32[1,1]{1,0:T(1,128)S(6)} %copy.13.count, bf16[64,64,128]{2,1,0:T(8,128)(2,1)S(1)} %get-tuple-element.7.x_ref, bf16[512,128,128]{2,1,0:T(8,128)(2,1)S(1)} %get-tuple-element.8.tiles_ref), custom_call_target="tpu_custom_call" | custom-call | tf_op jit(solution)/shard_map/forward/pallas_call | solution.py:70
  39.8 16.7 %user_sum.1 = (bf16[64,64,128]{2,1,0:T(8,128)(2,1)S(1)}, bf16[512,128,128]{2,1,0:T(8,128)(2,1)S(1)}) custom-call(s32[1,512]{1,0:T(1,128)S(1)} %copy-done, bf16[64,64,128]{2,1,0:T(8,128)(2,1)S(1)} %forward.1.part_ref), custom_call_target="tpu_custom_call" | custom-call | tf_op jit(solution)/shard_map/user_sum/pallas_call | solution.py:328
  56.5 3.4 %backward.1.part_ref = bf16[64,64,128]{2,1,0:T(8,128)(2,1)S(1)} custom-call(s32[1,512]{1,0:T(1,128)S(1)} %multiply_add_fusion.places, s32[1,1]{1,0:T(1,128)S(6)} %copy.13.count, bf16[64,64,128]{2,1,0:T(8,128)(2,1)S(1)} %get-tuple-element.9.x_ref, bf16[512,128,128]{2,1,0:T(8,128)(2,1)S(1)} %get-tuple-element.10.tiles_ref), custom_call_target="tpu_custom_call" | custom-call | tf_op jit(solution)/shard_map/backward/pallas_call | solution.py:70
  60.0 33.6 %finish.1 = f32[1024,64]{1,0:T(8,128)S(1)} custom-call(bf16[64,64,128]{2,1,0:T(8,128)(2,1)S(1)} %backward.1.part_ref, bf16[128,1024]{1,0:T(8,128)(2,1)S(1)} %get-tuple-element.16.lock_ref, f32[32,128]{1,0:T(8,128)S(1)} %get-tuple-element.11.stats_ref), custom_call_target="tpu_custom_call" | custom-call | tf_op jit(solution)/shard_map/finish/pallas_call | solution.py:328
  93.6 0.9 copy.10
  94.5 0.7 copy_bitcast_fusion
  (1 shorter events, 0.0 us)
Async XLA Ops:
  1.8 0.7 copy-start
